TPU v7x, 256 devices: a whole 4x4x8 slice. The times are simulated.
256 devices in a mesh: wide: 64 (over y, z, core), narrow: 4 (over x).
Axes of the slice: x: 4, y: 4, z: 8, core: 2. Of those that a mesh axis runs over, the one named last changes fastest.
Arguments:
- embedding: float32 [131072, 128], P(('wide', 'narrow'))
- tile_blocks: bfloat16 [64, 4, 22, 512, 512], P('wide', 'narrow'), may hold values from -0.125 to 0.125
- tile_row: int32 [64, 4, 22], P('wide', 'narrow'), may hold values from 0 to 3
- tile_col: int32 [64, 4, 22], P('wide', 'narrow'), may hold values from 0 to 63
- counts: int32 [64, 4], P('wide', 'narrow'), may hold values from 1 to 22, as said below
Outputs:
- orthonormal: float32 [131072, 128], P(('wide', 'narrow'))
Inputs may be any that keep to these rules, and one draw needn't show every extreme that they name: Slots 0 to counts[w, n] - 1 of device (w, n) hold its tiles, the others are unused; some device has all 22 slots live.
All inputs are finite; a program needn't handle non-finite values.
Results may differ from a plain program's by a relative error of at most 0.0036.
Values may be sent and summed in bfloat16 or wider, within the bound.
No kernel may reach another device: no remote copies, remote signals or barrier semaphores. Data moves between devices by JAX's collectives and lax.ppermute only.
A program may use at most 64 MiB of HBM per device.

v0:
```python
import jax
import jax.numpy as jnp
from jax import lax
from jax.sharding import PartitionSpec as P


def apply_operator(values_bf, tile_local, row_local, col_local, live_count):
    tile_size = tile_local.shape[1]
    width = values_bf.shape[1]
    rows_dev = values_bf.shape[0]
    slab_count = lax.axis_size("narrow") * rows_dev // tile_size
    slot_count = tile_local.shape[0]
    gathered = lax.all_gather(values_bf, "wide", axis=0, tiled=True)
    blocks = gathered.reshape(-1, tile_size, width)
    picked = jnp.take(blocks, col_local, axis=0)
    products = jnp.einsum("sij,sjk->sik", tile_local, picked, preferred_element_type=jnp.float32)
    slot_ids = jnp.arange(slot_count, dtype=jnp.int32)
    slab_ids = jnp.arange(slab_count, dtype=jnp.int32)
    onehot = ((row_local[None, :] == slab_ids[:, None]) & (slot_ids[None, :] < live_count)).astype(
        jnp.float32
    )
    partial_value = jnp.einsum("rs,sik->rik", onehot, products, precision=lax.Precision.HIGHEST)
    partial_value = partial_value.reshape(slab_count * tile_size, width)
    slab_total = lax.psum(partial_value, "narrow")
    return lax.dynamic_slice_in_dim(slab_total, lax.axis_index("narrow") * rows_dev, rows_dev, 0)


def local(embedding, tile_blocks, tile_row, tile_col, counts):
    tile_local = tile_blocks[0, 0]
    row_local = tile_row[0, 0]
    col_local = tile_col[0, 0]
    live_count = counts[0, 0]
    emb_bf = embedding.astype(jnp.bfloat16)
    first_order = apply_operator(emb_bf, tile_local, row_local, col_local, live_count)
    first_bf = first_order.astype(jnp.bfloat16)
    second = (
        2.0 * apply_operator(first_bf, tile_local, row_local, col_local, live_count) - embedding
    )
    spectral = 1.2661 * embedding - 1.1303 * first_order + 0.2715 * second
    gram_part = lax.dot_general(
        spectral, spectral, (((0,), (0,)), ((), ())), precision=lax.Precision.HIGHEST
    )
    gram_matrix = lax.psum(gram_part, ("wide", "narrow"))
    lower_factor = jnp.linalg.cholesky(gram_matrix)
    solved = jax.scipy.linalg.solve_triangular(lower_factor, spectral.T, lower=True)
    node_total = embedding.shape[0] * lax.axis_size("wide") * lax.axis_size("narrow")
    return solved.T * jnp.sqrt(jnp.float32(node_total))


def solution(mesh):
    placed = (
        P(("wide", "narrow"), None),
        P("wide", "narrow", None, None, None),
        P("wide", "narrow", None),
        P("wide", "narrow", None),
        P("wide", "narrow"),
    )
    return jax.shard_map(
        local, mesh=mesh, in_specs=placed, out_specs=P(("wide", "narrow"), None), check_vma=False
    )
```

profile of v0, /device:TPU:1, one launch (start us, length us, event | category | flops | bytes accessed | tf_op | source)
XLA Modules:
  0.0 617.0 jit_solution(5770539556316250015)
XLA Ops:
  6.5 1.6 convert_element_type.8
  8.2 0.0 all-reduce.4.cloned.1.call-start
  8.9 0.7 compare_select_fusion
  9.6 0.7 compare_and_fusion
  10.2 87.1 %all-gather.3.cloned.1.call-done = bf16[32768,128]{1,0:T(8,128)(2,1)} async-done(((bf16[512,128]{1,0:T(8,128)(2,1)}), bf16[32768,128]{1,0:T(8,128)(2,1)}) %all-gather.3.cloned.1.call-update) | async-done | bytes 8388624 | tf_op jit(solution)/shard_map/all_gather | solution.py:13
  97.3 4.5 gather_fusion
  101.8 11.3 %fusion.2 = f32[22,128,512]{2,1,0:T(8,128)} fusion(bf16[1,1,22,512,512]{4,3,2,1,0:T(8,128)(2,1)} %param.8, bf16[22,512,128]{2,1,0:T(8,128)(2,1)S(1)} %gather_fusion, pred[22]{0:T(512)(128)(4,1)S(1)} %compare_and_fusion), kind=kOutput, calls=%fused_computation.4 | convolution fusion | flops 1477836800 | bytes 20185110 | tf_op jit(solution)/shard_map/sij,sjk->sik/dot_general | solution.py:16
  113.1 6.5 %copy.12 = f32[22,128,512]{1,0,2:T(8,128)} copy(f32[22,128,512]{2,1,0:T(8,128)} %fusion.2) | data formatting | bytes 11534336 | tf_op jit(solution)/shard_map/sij,sjk->sik/dot_general | solution.py:16
  119.6 5.0 fusion.6
  124.6 1.0 copy.8
  125.6 0.0 all-gather.5.cloned.1.call-start
  125.7 45.8 %all-reduce.4.cloned.1.call-done = f32[2048,128]{1,0:T(8,128)} async-done(((f32[2048,128]{1,0:T(8,128)}), f32[2048,128]{1,0:T(8,128)}) %all-reduce.4.cloned.1.call-update) | async-done | bytes 1048592 | tf_op jit(solution)/shard_map/psum | solution.py:24
  171.5 1.6 dynamic-slice_convert_fusion
  173.2 0.2 all-reduce.6.cloned.1.call-start
  173.4 87.1 %all-gather.5.cloned.1.call-done = bf16[32768,128]{1,0:T(8,128)(2,1)} async-done(((bf16[512,128]{1,0:T(8,128)(2,1)}), bf16[32768,128]{1,0:T(8,128)(2,1)}) %all-gather.5.cloned.1.call-update) | async-done | bytes 8388624 | tf_op jit(solution)/shard_map/all_gather | solution.py:13
  260.5 4.5 gather_fusion.1
  265.0 11.3 %fusion = f32[22,128,512]{2,1,0:T(8,128)} fusion(bf16[1,1,22,512,512]{4,3,2,1,0:T(8,128)(2,1)} %param.8, bf16[22,512,128]{2,1,0:T(8,128)(2,1)S(1)} %gather_fusion.1, pred[22]{0:T(512)(128)(4,1)S(1)} %compare_and_fusion), kind=kOutput, calls=%fused_computation.2 | convolution fusion | flops 1477836800 | bytes 20185110 | tf_op jit(solution)/shard_map/sij,sjk->sik/dot_general | solution.py:16
  276.3 6.4 %copy.13 = f32[22,128,512]{1,0,2:T(8,128)} copy(f32[22,128,512]{2,1,0:T(8,128)} %fusion) | data formatting | bytes 11534336 | tf_op jit(solution)/shard_map/sij,sjk->sik/dot_general | solution.py:16
  282.7 5.1 fusion.4
  287.8 1.1 copy.9
  288.9 0.3 all-reduce.8.cloned.1.call-start
  289.2 45.6 %all-reduce.6.cloned.1.call-done = f32[2048,128]{1,0:T(8,128)} async-done(((f32[2048,128]{1,0:T(8,128)}), f32[2048,128]{1,0:T(8,128)}) %all-reduce.6.cloned.1.call-update) | async-done | bytes 1048592 | tf_op jit(solution)/shard_map/psum | solution.py:24
  334.8 1.1 multiply_add_fusion
  335.9 1.2 fusion.23
  337.1 247.6 %all-reduce.8.cloned.1.call-done = f32[128,128]{0,1:T(8,128)} async-done(((f32[128,128]{0,1:T(8,128)}), f32[128,128]{0,1:T(8,128)}) %all-reduce.8.cloned.1.call-update) | async-done | bytes 65552 | tf_op jit(solution)/shard_map/psum | solution.py:43
  584.7 0.9 copy.11
  585.6 0.9 fusion.16
  586.5 11.7 %cholesky.16 = f32[128,128]{1,0:T(8,128)S(1)} custom-call(f32[128,128]{1,0:T(8,128)S(1)} %fusion.16), custom_call_target="Cholesky" | custom-call | tf_op jit(solution)/shard_map/jit(cholesky)/cholesky | solution.py:44
  598.2 0.6 compare_reduce_fusion
  598.9 0.7 fusion.14
  599.5 9.8 %custom-call.7 = f32[1,128,128]{1,2,0:T(8,128)S(1)} custom-call(f32[1,128,128]{2,1,0:T(8,128)S(1)} %fusion.14), custom_call_target="InvertDiagBlocksLowerTriangular" | custom-call | tf_op jit(solution)/shard_map/jit(_solve_triangular)/triangular_solve | solution.py:45
  609.4 1.1 convolution_multiply_fusion
  (13 shorter events, 0.1 us)
Async XLA Ops:
  6.5 90.8 %all-gather.3.cloned.1.call-start = ((), (), s32[]{:S(2)}) async-start(), calls=%async_computation | async-start | bytes 8519680 | tf_op jit(solution)/shard_map/all_gather | solution.py:13
  8.2 163.4 %all-reduce.4.cloned.1.call-start = ((), (), s32[]{:S(2)}) async-start(), calls=%async_computation.1 | async-start | bytes 2097152 | tf_op jit(solution)/shard_map/psum | solution.py:24
  113.1 6.5 %copy-start.1 = (s32[1,1,22]{2,1,0:T(1,128)S(1)}, s32[1,1,22]{2,1,0:T(1,128)}, u32[]{:S(2)}) copy-start(s32[1,1,22]{2,1,0:T(1,128)} %param.9) | copy-start | bytes 268
  125.6 134.9 %all-gather.5.cloned.1.call-start = ((), (), s32[]{:S(2)}) async-start(), calls=%async_computation.2 | async-start | bytes 8519680 | tf_op jit(solution)/shard_map/all_gather | solution.py:13
  173.2 161.6 %all-reduce.6.cloned.1.call-start = ((), (), s32[]{:S(2)}) async-start(), calls=%async_computation.3 | async-start | bytes 2097152 | tf_op jit(solution)/shard_map/psum | solution.py:24
  282.7 52.1 %copy-start = (f32[512,128]{1,0:T(8,128)S(1)}, f32[512,128]{1,0:T(8,128)}, u32[]{:S(2)}) copy-start(f32[512,128]{1,0:T(8,128)} %param.7) | copy-start | bytes 786436
  288.9 295.8 %all-reduce.8.cloned.1.call-start = ((), (), s32[]{:S(2)}) async-start(), calls=%async_computation.4 | async-start | bytes 131072 | tf_op jit(solution)/shard_map/psum | solution.py:43
Sparse Core Ops, SparseCore 0:
  10.1 87.1 all-gather.2
  125.8 45.7 all-reduce.3
  174.3 86.1 all-gather.4
  289.0 45.7 all-reduce.5
  340.1 244.5 all-reduce.7
where the time goes:
time: 618 us; the launch traced here: 617 us
  waiting for transfers between devices  513 us (83%)
  matrix products  34.9 us (6%)
  other arithmetic  27.8 us (4%)
  local copies, waits for them, and re-layouts  26.5 us (4%)
  between operations  13.9 us (2%)
    psum x1, waiting for transfers between devices, local(): gram_matrix = lax.psum(gram_part, ('wide', 'narrow'))  248 us
    all_gather x2, waiting for transfers between devices, apply_operator(): gathered = lax.all_gather(values_bf, 'wide', axis=0, tiled=True)  174 us
    psum x2, waiting for transfers between devices, apply_operator(): slab_total = lax.psum(partial_value, 'narrow')  91.4 us
    dot_general x2, matrix products, apply_operator(): jnp.einsum('sij,sjk->sik', tile_local, picked, preferred_element_type=jnp...  22.5 us
    dot_general x2, local copies, waits for them, and re-layouts, apply_operator(): jnp.einsum('sij,sjk->sik', tile_local, picked, preferred_element_type=jnp...  12.9 us
    another operation x3, other arithmetic, local(): lower_factor = jnp.linalg.cholesky(gram_matrix)  12.4 us
  transfers between devices with their start and end apart: 5, of which 5 were waited for; matrix products, arithmetic and copies ran while one was open for 0% of the time, Pallas kernels for 0%

commit v1 on v0

--- a/solution.py
+++ b/solution.py
@@ -40,7 +40,7 @@
     gram_part = lax.dot_general(
         spectral, spectral, (((0,), (0,)), ((), ())), precision=lax.Precision.HIGHEST
     )
-    gram_matrix = lax.psum(gram_part, ("wide", "narrow"))
+    gram_matrix = lax.psum(lax.psum(gram_part, "narrow"), "wide")
     lower_factor = jnp.linalg.cholesky(gram_matrix)
     solved = jax.scipy.linalg.solve_triangular(lower_factor, spectral.T, lower=True)
     node_total = embedding.shape[0] * lax.axis_size("wide") * lax.axis_size("narrow")

time: 618 us -> 594 us (0.961)
  waiting for transfers between devices: 513 us -> 490 us
    psum x1 -> x2, waiting for transfers between devices: 248 us -> 224 us  [local(): gram_matrix = lax.psum(lax.psum(gram_part, 'narrow'), 'wide')]
  transfers between devices with their start and end apart: 5 -> 6, of which waited for: 5 -> 6; matrix products, arithmetic and copies ran while one was open for 0% -> 0% of each run, Pallas kernels for 0% -> 0%
where the time goes in v1:
time: 594 us
  waiting for transfers between devices  490 us (82%)
  matrix products  34.9 us (6%)
  other arithmetic  27.8 us (5%)
  local copies, waits for them, and re-layouts  26.5 us (4%)
  between operations  14.2 us (2%)
    psum x2, waiting for transfers between devices, local(): gram_matrix = lax.psum(lax.psum(gram_part, 'narrow'), 'wide')  224 us
    all_gather x2, waiting for transfers between devices, apply_operator(): gathered = lax.all_gather(values_bf, 'wide', axis=0, tiled=True)  174 us
    psum x2, waiting for transfers between devices, apply_operator(): slab_total = lax.psum(partial_value, 'narrow')  91.7 us
    dot_general x2, matrix products, apply_operator(): jnp.einsum('sij,sjk->sik', tile_local, picked, preferred_element_type=jnp...  22.5 us
    dot_general x2, local copies, waits for them, and re-layouts, apply_operator(): jnp.einsum('sij,sjk->sik', tile_local, picked, preferred_element_type=jnp...  12.9 us
    another operation x3, other arithmetic, local(): lower_factor = jnp.linalg.cholesky(gram_matrix)  12.4 us
  transfers between devices with their start and end apart: 6, of which 6 were waited for; matrix products, arithmetic and copies ran while one was open for 0% of the time, Pallas kernels for 0%

profile of v1, /device:TPU:1, one launch (start us, length us, event | category | flops | bytes accessed | tf_op | source)
XLA Modules:
  0.0 593.8 jit_solution(17378647761954434075)
XLA Ops:
  6.5 1.6 convert_element_type.8
  8.9 0.7 compare_select_fusion
  9.6 0.7 compare_and_fusion
  10.2 87.1 %all-gather.3.cloned.1.call-done = bf16[32768,128]{1,0:T(8,128)(2,1)} async-done(((bf16[512,128]{1,0:T(8,128)(2,1)}), bf16[32768,128]{1,0:T(8,128)(2,1)}) %all-gather.3.cloned.1.call-update) | async-done | bytes 8388624 | tf_op jit(solution)/shard_map/all_gather | solution.py:13
  97.3 4.5 gather_fusion
  101.8 11.3 %fusion.2 = f32[22,128,512]{2,1,0:T(8,128)} fusion(bf16[1,1,22,512,512]{4,3,2,1,0:T(8,128)(2,1)} %param.8, bf16[22,512,128]{2,1,0:T(8,128)(2,1)S(1)} %gather_fusion, pred[22]{0:T(512)(128)(4,1)S(1)} %compare_and_fusion), kind=kOutput, calls=%fused_computation.4 | convolution fusion | flops 1477836800 | bytes 20185110 | tf_op jit(solution)/shard_map/sij,sjk->sik/dot_general | solution.py:16
  113.1 6.5 %copy.12 = f32[22,128,512]{1,0,2:T(8,128)} copy(f32[22,128,512]{2,1,0:T(8,128)} %fusion.2) | data formatting | bytes 11534336 | tf_op jit(solution)/shard_map/sij,sjk->sik/dot_general | solution.py:16
  119.6 5.0 fusion.6
  124.6 1.0 copy.8
  125.6 0.0 all-gather.5.cloned.1.call-start
  125.7 45.8 %all-reduce.5.cloned.1.call-done = f32[2048,128]{1,0:T(8,128)} async-done(((f32[2048,128]{1,0:T(8,128)}), f32[2048,128]{1,0:T(8,128)}) %all-reduce.5.cloned.1.call-update) | async-done | bytes 1048592 | tf_op jit(solution)/shard_map/psum | solution.py:24
  171.5 1.6 dynamic-slice_convert_fusion
  173.2 0.2 all-reduce.7.cloned.1.call-start
  173.4 87.1 %all-gather.5.cloned.1.call-done = bf16[32768,128]{1,0:T(8,128)(2,1)} async-done(((bf16[512,128]{1,0:T(8,128)(2,1)}), bf16[32768,128]{1,0:T(8,128)(2,1)}) %all-gather.5.cloned.1.call-update) | async-done | bytes 8388624 | tf_op jit(solution)/shard_map/all_gather | solution.py:13
  260.5 4.5 gather_fusion.1
  265.0 11.3 %fusion = f32[22,128,512]{2,1,0:T(8,128)} fusion(bf16[1,1,22,512,512]{4,3,2,1,0:T(8,128)(2,1)} %param.8, bf16[22,512,128]{2,1,0:T(8,128)(2,1)S(1)} %gather_fusion.1, pred[22]{0:T(512)(128)(4,1)S(1)} %compare_and_fusion), kind=kOutput, calls=%fused_computation.2 | convolution fusion | flops 1477836800 | bytes 20185110 | tf_op jit(solution)/shard_map/sij,sjk->sik/dot_general | solution.py:16
  276.3 6.4 %copy.13 = f32[22,128,512]{1,0,2:T(8,128)} copy(f32[22,128,512]{2,1,0:T(8,128)} %fusion) | data formatting | bytes 11534336 | tf_op jit(solution)/shard_map/sij,sjk->sik/dot_general | solution.py:16
  282.7 5.1 fusion.4
  287.8 1.1 copy.9
  289.0 45.8 %all-reduce.7.cloned.1.call-done = f32[2048,128]{1,0:T(8,128)} async-done(((f32[2048,128]{1,0:T(8,128)}), f32[2048,128]{1,0:T(8,128)}) %all-reduce.7.cloned.1.call-update) | async-done | bytes 1048592 | tf_op jit(solution)/shard_map/psum | solution.py:24
  334.8 1.1 multiply_add_fusion
  335.9 1.2 fusion.23
  337.1 0.3 all-reduce.11.cloned.1.call-start
  337.4 46.9 %all-reduce.9.cloned.1.call-done = f32[128,128]{0,1:T(8,128)} async-done(((f32[128,128]{0,1:T(8,128)}), f32[128,128]{0,1:T(8,128)}) %all-reduce.9.cloned.1.call-update) | async-done | bytes 65552 | tf_op jit(solution)/shard_map/psum | solution.py:43
  384.3 176.9 %all-reduce.11.cloned.1.call-done = f32[128,128]{0,1:T(8,128)} async-done(((f32[128,128]{0,1:T(8,128)}), f32[128,128]{0,1:T(8,128)}) %all-reduce.11.cloned.1.call-update) | async-done | bytes 65552 | tf_op jit(solution)/shard_map/psum | solution.py:43
  561.2 0.9 copy.11
  562.1 0.9 fusion.16
  563.0 11.7 %cholesky.16 = f32[128,128]{1,0:T(8,128)S(1)} custom-call(f32[128,128]{1,0:T(8,128)S(1)} %fusion.16), custom_call_target="Cholesky" | custom-call | tf_op jit(solution)/shard_map/jit(cholesky)/cholesky | solution.py:44
  574.8 0.6 compare_reduce_fusion
  575.4 0.7 fusion.14
  576.1 9.8 %custom-call.7 = f32[1,128,128]{1,2,0:T(8,128)S(1)} custom-call(f32[1,128,128]{2,1,0:T(8,128)S(1)} %fusion.14), custom_call_target="InvertDiagBlocksLowerTriangular" | custom-call | tf_op jit(solution)/shard_map/jit(_solve_triangular)/triangular_solve | solution.py:45
  585.9 1.1 convolution_multiply_fusion
  (16 shorter events, 0.2 us)
Async XLA Ops:
  6.5 90.8 %all-gather.3.cloned.1.call-start = ((), (), s32[]{:S(2)}) async-start(), calls=%async_computation | async-start | bytes 8519680 | tf_op jit(solution)/shard_map/all_gather | solution.py:13
  8.2 163.4 %all-reduce.5.cloned.1.call-start = ((), (), s32[]{:S(2)}) async-start(), calls=%async_computation.1 | async-start | bytes 2097152 | tf_op jit(solution)/shard_map/psum | solution.py:24
  113.1 6.5 %copy-start.1 = (s32[1,1,22]{2,1,0:T(1,128)S(1)}, s32[1,1,22]{2,1,0:T(1,128)}, u32[]{:S(2)}) copy-start(s32[1,1,22]{2,1,0:T(1,128)} %param.9) | copy-start | bytes 268
  125.6 134.9 %all-gather.5.cloned.1.call-start = ((), (), s32[]{:S(2)}) async-start(), calls=%async_computation.2 | async-start | bytes 8519680 | tf_op jit(solution)/shard_map/all_gather | solution.py:13
  173.2 161.6 %all-reduce.7.cloned.1.call-start = ((), (), s32[]{:S(2)}) async-start(), calls=%async_computation.3 | async-start | bytes 2097152 | tf_op jit(solution)/shard_map/psum | solution.py:24
  282.7 52.1 %copy-start = (f32[512,128]{1,0:T(8,128)S(1)}, f32[512,128]{1,0:T(8,128)}, u32[]{:S(2)}) copy-start(f32[512,128]{1,0:T(8,128)} %param.7) | copy-start | bytes 786436
  288.9 95.4 %all-reduce.9.cloned.1.call-start = ((), (), s32[]{:S(2)}) async-start(), calls=%async_computation.4 | async-start | bytes 131072 | tf_op jit(solution)/shard_map/psum | solution.py:43
  337.1 224.1 %all-reduce.11.cloned.1.call-start = ((), (), s32[]{:S(2)}) async-start(), calls=%async_computation.5 | async-start | bytes 131072 | tf_op jit(solution)/shard_map/psum | solution.py:43
Sparse Core Ops, SparseCore 0:
  10.1 87.1 all-gather.2
  125.8 45.7 all-reduce.4
  174.3 86.1 all-gather.4
  289.0 45.7 all-reduce.6
  337.3 46.9 all-reduce.8
  387.6 173.5 all-reduce.10
